TPU v7x, 32 devices: a whole 2x2x4 slice. The times are simulated.
32 devices in a mesh: space: 8 (over z, core), tm: 4 (over y, x).
Axes of the slice: x: 2, y: 2, z: 4, core: 2. Of those that a mesh axis runs over, the one named last changes fastest.
Arguments:
- snapshots: bfloat16 [32768, 512], P('space', 'tm'), may hold values from -6 to 6
- stencil_starts: int32 [512], P('tm'), may hold values from 0 to 508, as said below
- stencil_widths: int32 [512], P('tm'), may hold values from 4 to 40, as said below
- stencil_coeffs: bfloat16 [512, 40], P('tm'), may hold values from -2 to 2
- panels: bfloat16 [512, 256], P('tm'), may hold values from -0.25 to 0.25
Outputs:
- gram: float32 [512, 512], P(('tm', 'space'))
- modes: bfloat16 [32768, 256], P(('space', 'tm'))
Inputs may be any that keep to these rules, and one draw needn't show every extreme that they name: `stencil_starts`: uniform time u's stencil starts inside its own time block, snapshots from (u // 128) * 128 to that plus 128 - 1, and ends before snapshot 512. `stencil_widths`: some stencil has width 40 and some has width 4.
All inputs are finite; a program needn't handle non-finite values.
Results may differ from a plain program's by a relative error of at most 0.0049.
Values may be sent and summed in bfloat16 or wider, within the bound.
A program may use at most 64 MiB of HBM per device.

v0:
```python
import jax
import jax.numpy as jnp
from jax import lax
from jax.sharding import PartitionSpec as P


def shifted(value, axis, steps):
    count = lax.axis_size(axis)
    initial, last = (max(0, -steps), min(count, count - steps))
    return lax.ppermute(value, axis, [(source, source + steps) for source in range(initial, last)])


def on_device(snapshots, stencil_starts, stencil_widths, stencil_coeffs, panels):
    rows, block = snapshots.shape
    width_max = stencil_coeffs.shape[1]
    rim = shifted(snapshots[:, : width_max - 1], "tm", -1)
    extended = jnp.concatenate([snapshots, rim], axis=1)
    offsets = stencil_starts - lax.axis_index("tm") * block
    position = jnp.arange(block + width_max - 1, dtype=jnp.int32)[:, None]
    relative = position - offsets[None, :]
    steps = jnp.arange(width_max, dtype=jnp.int32)[:, None, None]
    picked = (relative[None, :, :] == steps) & (steps < stencil_widths[None, None, :])
    coeff_table = stencil_coeffs.T[:, None, :].astype(jnp.float32)
    weights = jnp.sum(jnp.where(picked, coeff_table, 0.0), axis=0).astype(jnp.bfloat16)
    resampled = jnp.dot(extended, weights, preferred_element_type=jnp.float32).astype(jnp.bfloat16)
    scale = 1.0 / (rows * lax.axis_size("space"))
    share = rows // lax.axis_size("tm")
    whole = lax.all_gather(resampled, "tm", axis=1, tiled=True)
    partial_value = lax.dot_general(
        resampled, whole, (((0,), (0,)), ((), ())), preferred_element_type=jnp.float32
    )
    every_panel = lax.all_gather(panels, "tm", axis=0, tiled=True)
    mine = lax.dynamic_slice_in_dim(whole, lax.axis_index("tm") * share, share, 0)
    modes = jnp.dot(mine, every_panel, preferred_element_type=jnp.float32).astype(jnp.bfloat16)
    partial_value = partial_value * scale
    gram = lax.psum_scatter(partial_value, "space", scatter_dimension=0, tiled=True)
    return (gram, modes)


def solution(mesh):
    return jax.shard_map(
        on_device,
        mesh=mesh,
        in_specs=(P("space", "tm"), P("tm"), P("tm"), P("tm", None), P("tm", None)),
        out_specs=(P(("tm", "space"), None), P(("space", "tm"), None)),
        check_vma=False,
    )
```

profile of v0, /device:TPU:0, one launch (start us, length us, event | category | flops | bytes accessed | tf_op | source)
XLA Modules:
  0.0 120.7 jit_solution(11758978963417569077)
XLA Ops:
  7.2 0.0 all-gather.2.cloned.1.call-start
  7.2 1.6 %copy.11 = bf16[4096,39]{0,1:T(8,128)(2,1)S(1)} copy(bf16[4096,39]{1,0:T(8,128)(2,1)} %bitcast.7) | data formatting | bytes 638976
  8.8 1.3 %collective-permute-start = (bf16[4096,39]{0,1:T(8,128)(2,1)S(1)}, bf16[4096,39]{0,1:T(8,128)(2,1)S(1)}, u32[]{:S(2)}, u32[]{:S(2)}) collective-permute-start(bf16[4096,39]{0,1:T(8,128)(2,1)S(1)} %copy.11), channel_id=1, source_target_pairs={{1,0},{2,1},{3,2},{5,4},{6,5},{7,6},{9,8},{10,9},{11,10},{13,12},{... | collective-permute-start | bytes 958472 | tf_op jit(solution)/shard_map/ppermute | solution.py:10
  10.1 0.7 convert_bitcast_fusion
  10.8 0.7 broadcast_subtract_fusion
  11.5 0.7 iota_compare_fusion.1
  12.2 1.4 %select_reduce_fusion = bf16[167,128]{1,0:T(8,128)(2,1)S(1)} fusion(f32[40,128]{1,0:T(8,128)S(1)} %convert_bitcast_fusion, s32[167,128]{1,0:T(8,128)S(1)} %iota_subtract_fusion, pred[40,128]{1,0:T(8,128)(4,1)S(1)} %iota_compare_fusion.1), kind=kLoop, calls=%fused_computation.1 | loop fusion | flops 3398784 | bytes 153856 | tf_op jit(solution)/shard_map/reduce_sum | solution.py:24
  13.6 7.8 %collective-permute-done = bf16[4096,39]{0,1:T(8,128)(2,1)S(1)} collective-permute-done((bf16[4096,39]{0,1:T(8,128)(2,1)S(1)}, bf16[4096,39]{0,1:T(8,128)(2,1)S(1)}, u32[]{:S(2)}, u32[]{:S(2)}) %collective-permute-start) | collective-permute-done | bytes 319520 | tf_op jit(solution)/shard_map/ppermute | solution.py:10
  21.4 0.5 copy.10
  21.9 2.9 %convolution_convert_fusion = bf16[4096,128]{1,0:T(8,128)(2,1)} fusion(bf16[4096,39]{1,0:T(8,128)(2,1)S(1)} %copy.10, bf16[4096,128]{1,0:T(8,128)(2,1)} %param.5, bf16[167,128]{1,0:T(8,128)(2,1)S(1)} %select_reduce_fusion), kind=kOutput, calls=%fused_computation | convolution fusion | flops 178372608 | bytes 2459392 | tf_op jit(solution)/shard_map/dot_general | solution.py:25
  24.8 0.0 copy-start
  24.8 0.0 all-gather.2.cloned.1.call-update
  24.8 0.0 reduce-scatter.2.cloned.1.call-start
  24.9 54.0 %all-gather.2.cloned.1.call-done = bf16[4096,512]{1,0:T(8,128)(2,1)} async-done(((bf16[4096,128]{1,0:T(8,128)(2,1)}), bf16[4096,512]{1,0:T(8,128)(2,1)}) %all-gather.2.cloned.1.call-update) | async-done | bytes 4194320 | tf_op jit(solution)/shard_map/all_gather | solution.py:28
  78.9 4.0 %convolution_multiply_fusion = f32[128,512]{1,0:T(8,128)} fusion(bf16[4096,128]{1,0:T(8,128)(2,1)} %convolution_convert_fusion, bf16[4096,512]{1,0:T(8,128)(2,1)} %all-gather.2.cloned.1.call-done), kind=kOutput, calls=%fused_computation.8 | convolution fusion | flops 536936448 | bytes 5505024 | tf_op jit(solution)/shard_map/dot_general | solution.py:29
  82.8 0.0 reduce-scatter.2.cloned.1.call-update
  82.9 0.0 copy-done
  82.9 9.0 %all_gather.7 = bf16[512,256]{1,0:T(8,128)(2,1)S(1)} all-gather(bf16[128,256]{1,0:T(8,128)(2,1)S(1)} %copy-done), channel_id=1, replica_groups=mesh['space'=8,'tm'=4] {'tm'}, dimensions={0}, use_global_device_ids=true | all-gather | bytes 327680 | tf_op jit(solution)/shard_map/all_gather | solution.py:32
  91.9 2.5 %convolution_convert_fusion.1 = bf16[1024,256]{1,0:T(8,128)(2,1)} fusion(bf16[512,256]{1,0:T(8,128)(2,1)S(1)} %all_gather.7, bf16[4096,512]{1,0:T(8,128)(2,1)} %all-gather.2.cloned.1.call-done, s32[]{:T(128)S(6)} %select_n.8), kind=kOutput, calls=%fused_computation.7 | convolution fusion | flops 268697600 | bytes 1835012 | tf_op jit(solution)/shard_map/dot_general | solution.py:34
  94.3 19.6 %reduce-scatter.2.cloned.1.call-done = f32[16,512]{1,0:T(8,128)} async-done(((f32[128,512]{1,0:T(8,128)}), f32[16,512]{1,0:T(8,128)}) %reduce-scatter.2.cloned.1.call-update) | async-done | bytes 32784 | tf_op jit(solution)/shard_map/reduce_scatter | solution.py:36
  (1 shorter events, 0.0 us)
Async XLA Ops:
  7.2 71.7 %all-gather.2.cloned.1.call-start = ((), (), s32[]{:S(2)}) async-start(), calls=%async_computation.1 | async-start | bytes 5242880 | tf_op jit(solution)/shard_map/all_gather | solution.py:28
  8.8 12.6 %collective-permute-start = (bf16[4096,39]{0,1:T(8,128)(2,1)S(1)}, bf16[4096,39]{0,1:T(8,128)(2,1)S(1)}, u32[]{:S(2)}, u32[]{:S(2)}) collective-permute-start(bf16[4096,39]{0,1:T(8,128)(2,1)S(1)} %copy.11), channel_id=1, source_target_pairs={{1,0},{2,1},{3,2},{5,4},{6,5},{7,6},{9,8},{10,9},{11,10},{13,12},{... | collective-permute-start | bytes 958472 | tf_op jit(solution)/shard_map/ppermute | solution.py:10
  24.8 58.1 %copy-start = (bf16[128,256]{1,0:T(8,128)(2,1)S(1)}, bf16[128,256]{1,0:T(8,128)(2,1)}, u32[]{:S(2)}) copy-start(bf16[128,256]{1,0:T(8,128)(2,1)} %param.9) | copy-start | bytes 196612
  24.8 89.1 %reduce-scatter.2.cloned.1.call-start = ((), (), s32[]{:S(2)}) async-start(), calls=%async_computation.2 | async-start | bytes 294912 | tf_op jit(solution)/shard_map/reduce_scatter | solution.py:36
Sparse Core Ops, SparseCore 0:
  24.9 53.8 all-gather.1
  83.0 30.8 reduce-scatter.1
where the time goes:
time: 121 us
  waiting for transfers between devices  81.4 us (67%)
  between operations  14.1 us (12%)
  matrix products  9.31 us (8%)
  blocking collectives  9 us (7%)
  other arithmetic  3.49 us (3%)
  local copies, waits for them, and re-layouts  2.12 us (2%)
  starting transfers between devices  1.36 us (1%)
    all_gather x1, waiting for transfers between devices, on_device(): whole = lax.all_gather(resampled, 'tm', axis=1, tiled=True)  54 us
    reduce_scatter x1, waiting for transfers between devices, on_device(): lax.psum_scatter(partial_value, 'space', scatter_dimension=0, tiled=True)  19.6 us
    all_gather x1, blocking collectives, on_device(): every_panel = lax.all_gather(panels, 'tm', axis=0, tiled=True)  9 us
    ppermute x1, waiting for transfers between devices, shifted(): lax.ppermute(value, axis, [(source, source + steps) for source in range(i...  7.78 us
    dot_general x1, matrix products, on_device(): lax.dot_general(resampled, whole, (((0,), (0,)), ((), ())), preferred_ele...  3.97 us
    dot_general x1, matrix products, on_device(): jnp.dot(extended, weights, preferred_element_type=jnp.float32)  2.9 us
    dot_general x1, matrix products, on_device(): jnp.dot(mine, every_panel, preferred_element_type=jnp.float32)  2.45 us
  transfers between devices with their start and end apart: 3, of which 3 were waited for; matrix products, arithmetic and copies ran while one was open for 5% of the time, Pallas kernels for 0%

commit v1 on v0

v1 whole, which is shorter than its diff:
```python
import functools

import jax
import jax.numpy as jnp
from jax import lax
from jax.experimental import pallas as pl
from jax.experimental.pallas import tpu as pltpu
from jax.sharding import PartitionSpec as P

F32 = jnp.float32
BF16 = jnp.bfloat16
CORES = 2


def shifted(value, axis, steps):
    count = lax.axis_size(axis)
    initial, last = (max(0, -steps), min(count, count - steps))
    return lax.ppermute(value, axis, [(source, source + steps) for source in range(initial, last)])


def on_device(snapshots, stencil_starts, stencil_widths, stencil_coeffs, panels):
    rows, block = snapshots.shape
    width_max = stencil_coeffs.shape[1]
    rim = shifted(snapshots[:, : width_max - 1], "tm", -1)
    extended = jnp.concatenate([snapshots, rim], axis=1)
    offsets = stencil_starts - lax.axis_index("tm") * block
    position = jnp.arange(block + width_max - 1, dtype=jnp.int32)[:, None]
    relative = position - offsets[None, :]
    steps = jnp.arange(width_max, dtype=jnp.int32)[:, None, None]
    picked = (relative[None, :, :] == steps) & (steps < stencil_widths[None, None, :])
    coeff_table = stencil_coeffs.T[:, None, :].astype(F32)
    weights = jnp.sum(jnp.where(picked, coeff_table, 0.0), axis=0).astype(BF16)
    resampled = jnp.dot(extended, weights, preferred_element_type=F32).astype(BF16)
    scale = 1.0 / (rows * lax.axis_size("space"))
    share = rows // lax.axis_size("tm")
    whole = lax.all_gather(resampled, "tm", axis=1, tiled=True)
    partial_value = lax.dot_general(
        resampled, whole, (((0,), (0,)), ((), ())), preferred_element_type=F32
    )
    every_panel = lax.all_gather(panels, "tm", axis=0, tiled=True)
    mine = lax.dynamic_slice_in_dim(whole, lax.axis_index("tm") * share, share, 0)
    modes = jnp.dot(mine, every_panel, preferred_element_type=F32).astype(BF16)
    partial_value = partial_value * scale
    gram = lax.psum_scatter(partial_value, "space", scatter_dimension=0, tiled=True)
    return (gram, modes)


def spread(packed, width_max, block):
    table = packed.astype(F32)
    rows = table.shape[0]
    moved = table[width_max : width_max + 1, :].astype(jnp.int32)
    index = lax.broadcasted_iota(jnp.int32, table.shape, 0)
    value = jnp.where(index < width_max, table, 0.0)
    step = 1
    while step < block:
        chosen = (moved & step) != 0
        if step < 8:
            other = pltpu.roll(value, step, 0)
        else:
            empty = jnp.zeros((step, block), F32)
            other = jnp.concatenate([empty, value], axis=0)
            value = jnp.concatenate([value, empty], axis=0)
        value = jnp.where(jnp.broadcast_to(chosen, value.shape), other, value)
        step *= 2
    return value


def kernel(
    nsp, ntm, chunks, width_max,
    snap, starts, widths, coeffs, panels,
    gram_out, modes_out,
    packed, weights, gathered, resampled, acc, pair_in, mine32, tm_out, tm_in, z_out, z_in, panel_all, modes_buf,
    local_sem, pack_send, pack_recv, row_send, row_recv, panel_send, panel_recv,
    pair_send, pair_recv, tm_send, tm_recv, z_send, z_recv,
):
    space = lax.axis_index("space")
    t = lax.axis_index("tm")
    zz, core = space // CORES, space % CORES
    nz = nsp // CORES
    block = snap.shape[1]
    share = snap.shape[0] // ntm
    piece = share // chunks
    nu = block * ntm

    def at(space_id, tm_id):
        return dict(device_id=(space_id, tm_id), device_id_type=pl.DeviceIdType.MESH)

    tm_peers = [lax.rem(t + d, ntm) for d in range(1, ntm)]
    z_peers = [lax.rem(zz + d, nz) * CORES + core for d in range(1, nz)]
    partner = zz * CORES + (1 - core)

    barrier = pltpu.get_barrier_semaphore()
    for peer in z_peers:
        pl.semaphore_signal(barrier, inc=1, **at(peer, t))
    for peer in tm_peers:
        pl.semaphore_signal(barrier, inc=1, **at(space, peer))
    pl.semaphore_signal(barrier, inc=1, **at(partner, t))

    own_rows = pltpu.make_async_copy(
        snap.at[pl.ds(t * share, share), :],
        gathered.at[:, pl.ds(pl.multiple_of(t * block, block), block)],
        local_sem.at[0],
    )
    own_rows.start()
    own_panels = pltpu.make_async_copy(
        panels, panel_all.at[pl.ds(pl.multiple_of(t * block, block), block), :], local_sem.at[1]
    )
    own_panels.start()

    prow = packed.shape[1]
    unit = (
        lax.broadcasted_iota(jnp.int32, (prow, width_max), 0)
        == lax.broadcasted_iota(jnp.int32, (prow, width_max), 1)
    ).astype(F32).astype(BF16)
    turned = lax.dot_general(unit, coeffs[...], (((1,), (1,)), ((), ())), preferred_element_type=F32)
    index = lax.broadcasted_iota(jnp.int32, turned.shape, 0)
    offset = (starts[...] - t * block).astype(F32)
    table = jnp.where(index < jnp.broadcast_to(widths[...], turned.shape), turned, 0.0)
    table = jnp.where(index == width_max, jnp.broadcast_to(offset, turned.shape), table)
    packed[t] = table.astype(BF16)

    pl.semaphore_wait(barrier, len(z_peers) + len(tm_peers) + 1)

    sends = []
    for i, peer in enumerate(tm_peers):
        sends.append(pltpu.make_async_remote_copy(
            src_ref=packed.at[t], dst_ref=packed.at[t],
            send_sem=pack_send.at[i], recv_sem=pack_recv.at[i], **at(space, peer)))
        sends[-1].start()
    for c in range(chunks):
        for i, peer in enumerate(tm_peers):
            sends.append(pltpu.make_async_remote_copy(
                src_ref=snap.at[pl.ds(pl.multiple_of(peer * share + c * piece, piece), piece), :],
                dst_ref=gathered.at[pl.ds(c * piece, piece), pl.ds(pl.multiple_of(t * block, block), block)],
                send_sem=row_send.at[c, i], recv_sem=row_recv.at[c, i], **at(space, peer)))
            sends[-1].start()
    for i, peer in enumerate(tm_peers):
        sends.append(pltpu.make_async_remote_copy(
            src_ref=panels, dst_ref=panel_all.at[pl.ds(pl.multiple_of(t * block, block), block), :],
            send_sem=panel_send.at[i], recv_sem=panel_recv.at[i], **at(space, peer)))
        sends[-1].start()

    weights[...] = jnp.zeros_like(weights)
    acc[...] = jnp.zeros_like(acc)

    def arrival(dst, sem):
        return pltpu.make_async_remote_copy(
            src_ref=dst, dst_ref=dst, send_sem=sem, recv_sem=sem, **at(space, tm_peers[0]))

    def origin(i):
        return lax.rem(t + ntm - (i + 1), ntm)

    for i in range(ntm - 1):
        arrival(packed.at[origin(i)], pack_recv.at[i]).wait_recv()
    for b in range(ntm):
        value = spread(packed[b], width_max, block).astype(BF16)
        height = min(value.shape[0], nu - b * block)
        weights[b * block : b * block + height, b * block : (b + 1) * block] = value[:height]

    own_rows.wait()
    span = CORES * block

    def chunk_step(c, carry):
        at_rows = pl.ds(pl.multiple_of(c * piece, piece), piece)
        for i in range(ntm - 1):
            arrival(
                gathered.at[at_rows, pl.ds(pl.multiple_of(origin(i) * block, block), block)], row_recv.at[c, i]
            ).wait_recv()
        for first in range(0, nu, span):
            last = min(first + 2 * span, nu)
            part = jnp.dot(
                gathered[at_rows, first:last], weights[first:last, first : first + span],
                preferred_element_type=F32,
            )
            resampled[at_rows, first : first + span] = part.astype(BF16)
        rows = resampled[at_rows, :]
        acc[...] += lax.dot_general(
            rows, rows, (((0,), (0,)), ((), ())), preferred_element_type=F32
        ).reshape(acc.shape)
        return carry

    lax.fori_loop(0, chunks, chunk_step, 0)

    pair = pltpu.make_async_remote_copy(
        src_ref=acc.at[:, 1 - core], dst_ref=pair_in,
        send_sem=pair_send, recv_sem=pair_recv, **at(partner, t))
    pair.start()

    own_panels.wait()
    for i in range(ntm - 1):
        arrival(panel_all.at[pl.ds(pl.multiple_of(origin(i) * block, block), block), :], panel_recv.at[i]).wait_recv()

    def modes_step(c, carry):
        at_rows = pl.ds(pl.multiple_of(c * piece, piece), piece)
        modes_buf[at_rows, :] = jnp.dot(
            resampled[at_rows, :], panel_all[...], preferred_element_type=F32).astype(BF16)
        return carry

    pair.wait_recv()
    summed = acc[:, pl.ds(core, 1)].reshape(pair_in.shape) + pair_in[...]
    summed = summed.reshape(mine32.shape)
    mine32[...] = summed
    tm_out[...] = summed.astype(BF16)
    for i, peer in enumerate(tm_peers):
        sends.append(pltpu.make_async_remote_copy(
            src_ref=tm_out.at[peer], dst_ref=tm_in.at[i],
            send_sem=tm_send.at[i], recv_sem=tm_recv.at[i], **at(space, peer)))
        sends[-1].start()
    lax.fori_loop(0, chunks, modes_step, 0)
    modes_copy = pltpu.make_async_copy(modes_buf, modes_out, local_sem.at[2])
    modes_copy.start()
    total = mine32[t]
    for i in range(ntm - 1):
        arrival(tm_in.at[i], tm_recv.at[i]).wait_recv()
        total = total + tm_in[i].astype(F32)
    mine32[t] = total
    z_out[...] = total.astype(BF16)
    for i, peer in enumerate(z_peers):
        sends.append(pltpu.make_async_remote_copy(
            src_ref=z_out.at[lax.rem(zz + i + 1, nz)], dst_ref=z_in.at[i],
            send_sem=z_send.at[i], recv_sem=z_recv.at[i], **at(peer, t)))
        sends[-1].start()
    final = mine32[t, zz]
    for i in range(nz - 1):
        arrival(z_in.at[i], z_recv.at[i]).wait_recv()
        final = final + z_in[i].astype(F32)
    gram_out[...] = final * (1.0 / (snap.shape[0] * nsp))

    pair.wait_send()
    for copy in sends:
        copy.wait_send()
    modes_copy.wait()


def fused(nsp, ntm, snapshots, stencil_starts, stencil_widths, stencil_coeffs, panels):
    rows, block = snapshots.shape
    width_max = stencil_coeffs.shape[1]
    nmode = panels.shape[1]
    nu, share, nz = block * ntm, rows // ntm, nsp // CORES
    own = nu // (ntm * nsp)
    chunks = 4
    prow = -(-(width_max + 1) // 16) * 16
    vmem = pl.BlockSpec(memory_space=pltpu.VMEM)
    hbm = pl.BlockSpec(memory_space=pl.ANY)
    dma = pltpu.SemaphoreType.DMA
    call = pl.pallas_call(
        functools.partial(kernel, nsp, ntm, chunks, width_max),
        out_shape=(
            jax.ShapeDtypeStruct((own, nu), F32),
            jax.ShapeDtypeStruct((share, nmode), BF16),
        ),
        in_specs=[hbm, vmem, vmem, vmem, vmem],
        out_specs=(vmem, hbm),
        scratch_shapes=[
            pltpu.VMEM((ntm, prow, block), BF16),
            pltpu.VMEM((nu, nu), BF16),
            pltpu.VMEM((share, nu), BF16),
            pltpu.VMEM((share, nu), BF16),
            pltpu.VMEM((ntm * nz, CORES, own, nu), F32),
            pltpu.VMEM((ntm * nz, own, nu), F32),
            pltpu.VMEM((ntm, nz, own, nu), F32),
            pltpu.VMEM((ntm, nz, own, nu), BF16),
            pltpu.VMEM((ntm - 1, nz, own, nu), BF16),
            pltpu.VMEM((nz, own, nu), BF16),
            pltpu.VMEM((nz - 1, own, nu), BF16),
            pltpu.VMEM((nu, nmode), BF16),
            pltpu.VMEM((share, nmode), BF16),
            dma((3,)),
            dma((ntm - 1,)),
            dma((ntm - 1,)),
            dma((chunks, ntm - 1)),
            dma((chunks, ntm - 1)),
            dma((ntm - 1,)),
            dma((ntm - 1,)),
            dma,
            dma,
            dma((ntm - 1,)),
            dma((ntm - 1,)),
            dma((nz - 1,)),
            dma((nz - 1,)),
        ],
        compiler_params=pltpu.CompilerParams(
            collective_id=0, has_side_effects=True, vmem_limit_bytes=48 * 1024 * 1024
        ),
    )
    return call(
        snapshots, stencil_starts.reshape(1, block), stencil_widths.reshape(1, block), stencil_coeffs, panels
    )


def solution(mesh):
    nsp, ntm = mesh.shape["space"], mesh.shape["tm"]

    def body(snapshots, stencil_starts, stencil_widths, stencil_coeffs, panels):
        rows, block = snapshots.shape
        own = block // nsp
        fits = block == 128 and own % 16 == 0 and nsp % CORES == 0 and ntm % 2 == 0 and rows % (64 * ntm) == 0
        if fits and 4 * (block * ntm) ** 2 <= 4 * 1024 * 1024:
            return fused(nsp, ntm, snapshots, stencil_starts, stencil_widths, stencil_coeffs, panels)
        return on_device(snapshots, stencil_starts, stencil_widths, stencil_coeffs, panels)

    return jax.shard_map(
        body,
        mesh=mesh,
        in_specs=(P("space", "tm"), P("tm"), P("tm"), P("tm", None), P("tm", None)),
        out_specs=(P(("tm", "space"), None), P(("space", "tm"), None)),
        check_vma=False,
    )
```

time: 121 us -> 36.4 us (0.30)
  waiting for transfers between devices: 81.4 us -> 0 us
  Pallas kernels: 0 us -> 31.2 us
  between operations: 14.1 us -> 0.68 us
  matrix products: 9.31 us -> 0 us
  blocking collectives: 9 us -> 0 us
  other arithmetic: 3.49 us -> 0 us
  local copies, waits for them, and re-layouts: 2.12 us -> 4.3 us
  starting transfers between devices: 1.36 us -> 0 us
    all_gather x1 -> x0, waiting for transfers between devices: 54 us -> none  [on_device(): whole = lax.all_gather(resampled, 'tm', axis=1, tiled=True)]
    pallas_call x0 -> x1, Pallas kernels: none -> 31.2 us  [fused(): call(snapshots, stencil_starts.reshape(1, block), stencil_widths.reshape(...]
    reduce_scatter x1 -> x0, waiting for transfers between devices: 19.6 us -> none  [on_device(): lax.psum_scatter(partial_value, 'space', scatter_dimension=0, tiled=True)]
    dot_general x3 -> x0, matrix products: 9.31 us -> none  [the longest x1 3.97 us: on_device(): lax.dot_general(resampled, whole, (((0,), (0,)), ((), ())), preferred_ele...]
    all_gather x1 -> x0, blocking collectives: 9 us -> none  [on_device(): every_panel = lax.all_gather(panels, 'tm', axis=0, tiled=True)]
    ppermute x1 -> x0, waiting for transfers between devices: 7.78 us -> none  [shifted(): lax.ppermute(value, axis, [(source, source + steps) for source in range(i...]
    unnamed x3 -> x11, local copies, waits for them, and re-layouts: 1.63 us -> 4.3 us
    reduce_sum x1 -> x0, other arithmetic: 1.45 us -> none  [on_device(): jnp.sum(jnp.where(picked, coeff_table, 0.0), axis=0).astype(jnp.bfloat16)]
  transfers between devices with their start and end apart: 3 -> 0, of which waited for: 3 -> 0; matrix products, arithmetic and copies ran while one was open for 5% -> 0% of each run, Pallas kernels for 0% -> 0%
where the time goes in v1:
time: 36.4 us; the launch traced here: 36.2 us
  Pallas kernels  31.2 us (86%)
  local copies, waits for them, and re-layouts  4.3 us (12%)
  between operations  0.68 us (2%)
    pallas_call x1, Pallas kernels, fused(): call(snapshots, stencil_starts.reshape(1, block), stencil_widths.reshape(...  31.2 us
    unnamed x11, local copies, waits for them, and re-layouts  4.3 us

profile of v1, /device:TPU:0, one launch (start us, length us, event | category | flops | bytes accessed | tf_op | source)
XLA Modules:
  0.0 36.2 jit_solution(3692112813047279593)
XLA Ops:
  0.6 0.0 copy-start.2
  0.6 0.0 copy-start.3
  0.7 0.8 %copy.7.coeffs = bf16[128,40]{1,0:T(8,128)(2,1)S(1)} copy(bf16[128,40]{0,1:T(8,128)(2,1)} %param.8) | data formatting | bytes 20480 | tf_op args[3]
  1.5 0.0 copy-done.2
  1.5 0.0 copy-done.3
  1.5 0.0 copy-start
  1.5 1.2 %copy-done = bf16[4096,128]{1,0:T(8,128)(2,1)S(1)} copy-done((bf16[4096,128]{1,0:T(8,128)(2,1)S(1)}, bf16[4096,128]{1,0:T(8,128)(2,1)}, u32[]{:S(2)}) %copy-start) | copy-done | bytes 1048600
  2.7 0.0 copy-start.1
  2.7 0.8 %copy-done.1 = bf16[128,256]{1,0:T(8,128)(2,1)S(1)} copy-done((bf16[128,256]{1,0:T(8,128)(2,1)S(1)}, bf16[128,256]{1,0:T(8,128)(2,1)}, u32[]{:S(2)}) %copy-start.1) | copy-done | bytes 65560
  3.6 31.2 %shard_map.68 = (f32[16,512]{1,0:T(8,128)S(1)}, bf16[1024,256]{1,0:T(8,128)(2,1)S(1)}) custom-call(bf16[4096,128]{1,0:T(8,128)(2,1)S(1)} %copy-done, s32[1,128]{1,0:T(1,128)S(1)} %bitcast.2, s32[1,128]{1,0:T(1,128)S(1)} %bitcast.3, bf16[128,40]{1,0:T(8,128)(2,1)S(1)} %copy.7.coeffs, bf16[128,256]{1,0:T(8,128)(2,1)S(1)} %copy-done.1), custom_call_target="tpu_custom_call" | custom-call | tf_op jit(solution)/shard_map/pallas_call | solution.py:286
  34.8 0.6 %copy.10 = f32[16,512]{1,0:T(8,128)} copy(f32[16,512]{1,0:T(8,128)S(1)} %get-tuple-element.4) | data formatting | bytes 65536
  35.4 0.8 %copy.11 = bf16[1024,256]{1,0:T(8,128)(2,1)} copy(bf16[1024,256]{1,0:T(8,128)(2,1)S(1)} %get-tuple-element.5) | data formatting | bytes 1048576
Async XLA Ops:
  0.6 0.8 %copy-start.2 = (s32[128]{0:T(128)S(1)}, s32[128]{0:T(128)}, u32[]{:S(2)}) copy-start(s32[128]{0:T(128)} %param.6) | copy-start | bytes 1540
  0.6 0.8 %copy-start.3 = (s32[128]{0:T(128)S(1)}, s32[128]{0:T(128)}, u32[]{:S(2)}) copy-start(s32[128]{0:T(128)} %param.7) | copy-start | bytes 1540
  1.5 1.2 %copy-start = (bf16[4096,128]{1,0:T(8,128)(2,1)S(1)}, bf16[4096,128]{1,0:T(8,128)(2,1)}, u32[]{:S(2)}) copy-start(bf16[4096,128]{1,0:T(8,128)(2,1)} %snap.1) | copy-start | bytes 3145732
  2.7 0.8 %copy-start.1 = (bf16[128,256]{1,0:T(8,128)(2,1)S(1)}, bf16[128,256]{1,0:T(8,128)(2,1)}, u32[]{:S(2)}) copy-start(bf16[128,256]{1,0:T(8,128)(2,1)} %panels.1) | copy-start | bytes 196612

commit v2 on v1

v2 whole, which is shorter than its diff:
```python
import functools

import jax
import jax.numpy as jnp
from jax import lax
from jax.experimental import pallas as pl
from jax.experimental.pallas import tpu as pltpu
from jax.sharding import PartitionSpec as P

F32 = jnp.float32
BF16 = jnp.bfloat16
CORES = 2
CHUNKS = 8


def shifted(value, axis, steps):
    count = lax.axis_size(axis)
    initial, last = (max(0, -steps), min(count, count - steps))
    return lax.ppermute(value, axis, [(source, source + steps) for source in range(initial, last)])


def on_device(snapshots, stencil_starts, stencil_widths, stencil_coeffs, panels):
    rows, block = snapshots.shape
    width_max = stencil_coeffs.shape[1]
    rim = shifted(snapshots[:, : width_max - 1], "tm", -1)
    extended = jnp.concatenate([snapshots, rim], axis=1)
    offsets = stencil_starts - lax.axis_index("tm") * block
    position = jnp.arange(block + width_max - 1, dtype=jnp.int32)[:, None]
    relative = position - offsets[None, :]
    steps = jnp.arange(width_max, dtype=jnp.int32)[:, None, None]
    picked = (relative[None, :, :] == steps) & (steps < stencil_widths[None, None, :])
    coeff_table = stencil_coeffs.T[:, None, :].astype(F32)
    weights = jnp.sum(jnp.where(picked, coeff_table, 0.0), axis=0).astype(BF16)
    resampled = jnp.dot(extended, weights, preferred_element_type=F32).astype(BF16)
    scale = 1.0 / (rows * lax.axis_size("space"))
    share = rows // lax.axis_size("tm")
    whole = lax.all_gather(resampled, "tm", axis=1, tiled=True)
    partial_value = lax.dot_general(
        resampled, whole, (((0,), (0,)), ((), ())), preferred_element_type=F32
    )
    every_panel = lax.all_gather(panels, "tm", axis=0, tiled=True)
    mine = lax.dynamic_slice_in_dim(whole, lax.axis_index("tm") * share, share, 0)
    modes = jnp.dot(mine, every_panel, preferred_element_type=F32).astype(BF16)
    partial_value = partial_value * scale
    gram = lax.psum_scatter(partial_value, "space", scatter_dimension=0, tiled=True)
    return (gram, modes)


def spread(packed, width_max, block):
    table = packed.astype(F32)
    rows = table.shape[0]
    moved = table[width_max : width_max + 1, :].astype(jnp.int32)
    index = lax.broadcasted_iota(jnp.int32, table.shape, 0)
    value = jnp.where(index < width_max, table, 0.0)
    step = 1
    while step < block:
        chosen = (moved & step) != 0
        if step < 8:
            other = pltpu.roll(value, step, 0)
        else:
            empty = jnp.zeros((step, block), F32)
            other = jnp.concatenate([empty, value], axis=0)
            value = jnp.concatenate([value, empty], axis=0)
        value = jnp.where(jnp.broadcast_to(chosen, value.shape), other, value)
        step *= 2
    return value


def kernel(
    nsp, ntm, chunks, halves, width_max,
    snap, starts_in, widths_in, coeffs_in, panels,
    gram_out, modes_out,
    starts, widths, coeffs,
    packed, weights, gathered, resampled, acc, pair_in, mine32, tm_out, tm_in, z_out, z_in, panel_all,
    local_sem, pack_send, pack_recv, row_send, row_recv, panel_send, panel_recv,
    pair_send, pair_recv, tm_send, tm_recv, z_send, z_recv,
):
    space = lax.axis_index("space")
    t = lax.axis_index("tm")
    zz, core = space // CORES, space % CORES
    nz = nsp // CORES
    block = snap.shape[1]
    share = snap.shape[0] // ntm
    piece = share // chunks
    nu = block * ntm
    wide = nu // halves

    def at(space_id, tm_id):
        return dict(device_id=(space_id, tm_id), device_id_type=pl.DeviceIdType.MESH)

    tm_peers = [lax.rem(t + d, ntm) for d in range(1, ntm)]
    z_peers = [lax.rem(zz + d, nz) * CORES + core for d in range(1, nz)]
    partner = zz * CORES + (1 - core)

    barrier = pltpu.get_barrier_semaphore()
    for peer in z_peers:
        pl.semaphore_signal(barrier, inc=1, **at(peer, t))
    for peer in tm_peers:
        pl.semaphore_signal(barrier, inc=1, **at(space, peer))
    pl.semaphore_signal(barrier, inc=1, **at(partner, t))

    columns = pl.ds(pl.multiple_of(t * block, block), block)
    small = [
        pltpu.make_async_copy(source, target, local_sem.at[i])
        for i, (source, target) in enumerate(
            [(starts_in, starts), (widths_in, widths), (coeffs_in, coeffs)]
        )
    ]
    own_rows = pltpu.make_async_copy(
        snap.at[pl.ds(pl.multiple_of(t * share, share), share), :], gathered.at[:, columns], local_sem.at[3]
    )
    own_panels = pltpu.make_async_copy(panels, panel_all.at[columns, :], local_sem.at[4])
    for copy in small:
        copy.start()
    own_rows.start()
    own_panels.start()

    for copy in small:
        copy.wait()
    prow = packed.shape[1]
    turned = jnp.concatenate(
        [coeffs[...].astype(F32), jnp.zeros((prow - width_max, block), F32)], axis=0
    )
    index = lax.broadcasted_iota(jnp.int32, turned.shape, 0)
    offset = (starts[...] - t * block).astype(F32)
    table = jnp.where(index < jnp.broadcast_to(widths[...], turned.shape), turned, 0.0)
    table = jnp.where(index == width_max, jnp.broadcast_to(offset, turned.shape), table)
    packed[t] = table.astype(BF16)

    pl.semaphore_wait(barrier, len(z_peers) + len(tm_peers) + 1)

    sends = []

    def send(src, dst, send_sem, recv_sem, space_id, tm_id):
        copy = pltpu.make_async_remote_copy(
            src_ref=src, dst_ref=dst, send_sem=send_sem, recv_sem=recv_sem, **at(space_id, tm_id))
        copy.start()
        sends.append(copy)

    for i, peer in enumerate(tm_peers):
        send(packed.at[t], packed.at[t], pack_send.at[i], pack_recv.at[i], space, peer)
    for c in range(chunks):
        for i, peer in enumerate(tm_peers):
            send(
                snap.at[pl.ds(pl.multiple_of(peer * share + c * piece, piece), piece), :],
                gathered.at[pl.ds(c * piece, piece), columns],
                row_send.at[c, i], row_recv.at[c, i], space, peer)
    for i, peer in enumerate(tm_peers):
        send(panels, panel_all.at[columns, :], panel_send.at[i], panel_recv.at[i], space, peer)

    weights[...] = jnp.zeros_like(weights)
    acc[...] = jnp.zeros_like(acc)

    def arrived(dst, sem):
        pltpu.make_async_remote_copy(
            src_ref=dst, dst_ref=dst, send_sem=sem, recv_sem=sem, **at(space, tm_peers[0])
        ).wait_recv()

    origins = [lax.rem(t + ntm - d, ntm) for d in range(1, ntm)]

    for i, origin in enumerate(origins):
        arrived(packed.at[origin], pack_recv.at[i])
    for b in range(ntm):
        value = spread(packed[b], width_max, block).astype(BF16)
        height = min(value.shape[0], nu - b * block)
        weights[b * block : b * block + height, b * block : (b + 1) * block] = value[:height]

    own_rows.wait()
    span = CORES * block

    def resample(c):
        at_rows = pl.ds(pl.multiple_of(c * piece, piece), piece)
        for i, origin in enumerate(origins):
            arrived(
                gathered.at[at_rows, pl.ds(pl.multiple_of(origin * block, block), block)], row_recv.at[c, i]
            )
        for first in range(0, nu, span):
            last = min(first + 2 * span, nu)
            part = jnp.dot(
                gathered[at_rows, first:last], weights[first:last, first : first + span],
                preferred_element_type=F32,
            )
            resampled[at_rows, first : first + span] = part.astype(BF16)
        return resampled[at_rows, :]

    def product(left, right):
        value = lax.dot_general(left, right, (((0,), (0,)), ((), ())), preferred_element_type=F32)
        return value.reshape(acc.shape[:3] + (right.shape[1],))

    def chunk_step(c, carry):
        rows = resample(c)
        acc[...] += product(rows, rows)
        return carry

    lax.fori_loop(0, chunks - 1, chunk_step, 0)
    parts = [slice(h * wide, (h + 1) * wide) for h in range(halves)]
    rows = resample(chunks - 1)
    for h, part in enumerate(parts):
        acc[:, :, :, part] += product(rows, rows[:, part])
        send(acc.at[:, 1 - core, :, part], pair_in.at[:, :, part], pair_send.at[h], pair_recv.at[h], partner, t)

    for h, part in enumerate(parts):
        arrived(pair_in.at[:, :, part], pair_recv.at[h])
        summed = acc[:, pl.ds(core, 1), :, part].reshape(pair_in.shape[:2] + (wide,)) + pair_in[:, :, part]
        summed = summed.reshape(mine32.shape[:3] + (wide,))
        mine32[:, :, :, part] = summed
        tm_out[:, :, :, part] = summed.astype(BF16)
        for i, peer in enumerate(tm_peers):
            send(
                tm_out.at[peer, :, :, part], tm_in.at[i, :, :, part],
                tm_send.at[h, i], tm_recv.at[h, i], space, peer)

    own_panels.wait()
    for i, origin in enumerate(origins):
        arrived(panel_all.at[pl.ds(pl.multiple_of(origin * block, block), block), :], panel_recv.at[i])

    def modes_step(c, carry):
        at_rows = pl.ds(pl.multiple_of(c * piece, piece), piece)
        modes_out[at_rows, :] = jnp.dot(
            resampled[at_rows, :], panel_all[...], preferred_element_type=F32).astype(BF16)
        return carry

    lax.fori_loop(0, chunks, modes_step, 0)

    for h, part in enumerate(parts):
        total = mine32[pl.ds(t, 1), :, :, part].reshape(z_out.shape[:2] + (wide,))
        for i in range(ntm - 1):
            arrived(tm_in.at[i, :, :, part], tm_recv.at[h, i])
            total = total + tm_in[i, :, :, part].astype(F32)
        mine32[pl.ds(t, 1), :, :, part] = total[None]
        z_out[:, :, part] = total.astype(BF16)
        for i, peer in enumerate(z_peers):
            send(
                z_out.at[lax.rem(zz + i + 1, nz), :, part], z_in.at[i, :, part],
                z_send.at[h, i], z_recv.at[h, i], peer, t)
    for h, part in enumerate(parts):
        final = mine32[pl.ds(t, 1), pl.ds(zz, 1), :, part].reshape(gram_out.shape[0], wide)
        for i in range(nz - 1):
            arrived(z_in.at[i, :, part], z_recv.at[h, i])
            final = final + z_in[i, :, part].astype(F32)
        gram_out[:, part] = final * (1.0 / (snap.shape[0] * nsp))

    for copy in sends:
        copy.wait_send()


def fused(nsp, ntm, snapshots, stencil_starts, stencil_widths, stencil_coeffs, panels):
    rows, block = snapshots.shape
    width_max = stencil_coeffs.shape[1]
    nmode = panels.shape[1]
    nu, share, nz = block * ntm, rows // ntm, nsp // CORES
    own = nu // (ntm * nsp)
    chunks, halves = CHUNKS, 2
    prow = -(-(width_max + 1) // 16) * 16
    vmem = pl.BlockSpec(memory_space=pltpu.VMEM)
    hbm = pl.BlockSpec(memory_space=pltpu.HBM)
    dma = pltpu.SemaphoreType.DMA
    call = pl.pallas_call(
        functools.partial(kernel, nsp, ntm, chunks, halves, width_max),
        out_shape=(
            jax.ShapeDtypeStruct((own, nu), F32),
            jax.ShapeDtypeStruct((share, nmode), BF16),
        ),
        in_specs=[hbm, hbm, hbm, hbm, hbm],
        out_specs=(vmem, vmem),
        scratch_shapes=[
            pltpu.VMEM((1, block), jnp.int32),
            pltpu.VMEM((1, block), jnp.int32),
            pltpu.VMEM((width_max, block), BF16),
            pltpu.VMEM((ntm, prow, block), BF16),
            pltpu.VMEM((nu, nu), BF16),
            pltpu.VMEM((share, nu), BF16),
            pltpu.VMEM((share, nu), BF16),
            pltpu.VMEM((ntm * nz, CORES, own, nu), F32),
            pltpu.VMEM((ntm * nz, own, nu), F32),
            pltpu.VMEM((ntm, nz, own, nu), F32),
            pltpu.VMEM((ntm, nz, own, nu), BF16),
            pltpu.VMEM((ntm - 1, nz, own, nu), BF16),
            pltpu.VMEM((nz, own, nu), BF16),
            pltpu.VMEM((nz - 1, own, nu), BF16),
            pltpu.VMEM((nu, nmode), BF16),
            dma((5,)),
            dma((ntm - 1,)),
            dma((ntm - 1,)),
            dma((chunks, ntm - 1)),
            dma((chunks, ntm - 1)),
            dma((ntm - 1,)),
            dma((ntm - 1,)),
            dma((halves,)),
            dma((halves,)),
            dma((halves, ntm - 1)),
            dma((halves, ntm - 1)),
            dma((halves, nz - 1)),
            dma((halves, nz - 1)),
        ],
        compiler_params=pltpu.CompilerParams(
            collective_id=0, has_side_effects=True, vmem_limit_bytes=48 * 1024 * 1024
        ),
    )
    operands = (
        snapshots, stencil_starts.reshape(1, block), stencil_widths.reshape(1, block), stencil_coeffs.T, panels
    )
    return call(*(pltpu.with_memory_space_constraint(operand, pltpu.HBM) for operand in operands))


def solution(mesh):
    nsp, ntm = mesh.shape["space"], mesh.shape["tm"]

    def body(snapshots, stencil_starts, stencil_widths, stencil_coeffs, panels):
        rows, block = snapshots.shape
        own = block // nsp
        fits = block == 128 and own % 16 == 0 and nsp % CORES == 0 and ntm % 2 == 0 and rows % (64 * ntm) == 0
        if fits and 4 * (block * ntm) ** 2 <= 4 * 1024 * 1024:
            return fused(nsp, ntm, snapshots, stencil_starts, stencil_widths, stencil_coeffs, panels)
        return on_device(snapshots, stencil_starts, stencil_widths, stencil_coeffs, panels)

    return jax.shard_map(
        body,
        mesh=mesh,
        in_specs=(P("space", "tm"), P("tm"), P("tm"), P("tm", None), P("tm", None)),
        out_specs=(P(("tm", "space"), None), P(("space", "tm"), None)),
        check_vma=False,
    )
```

time: 36.4 us -> 32.1 us (0.88)
  local copies, waits for them, and re-layouts: 4.3 us -> 1.41 us
  Pallas kernels: 31.2 us -> 29.9 us
    unnamed x11 -> x2, local copies, waits for them, and re-layouts: 4.3 us -> 1.41 us
    pallas_call x1, Pallas kernels: 31.2 us -> 29.9 us  [fused(): call(*(pltpu.with_memory_space_constraint(operand, pltpu.HBM) for operand...]
where the time goes in v2:
time: 32.1 us; the launch traced here: 31.9 us
  Pallas kernels  29.9 us (93%)
  local copies, waits for them, and re-layouts  1.41 us (4%)
  between operations  0.64 us (2%)
    pallas_call x1, Pallas kernels, fused(): call(*(pltpu.with_memory_space_constraint(operand, pltpu.HBM) for operand...  29.9 us
    unnamed x2, local copies, waits for them, and re-layouts  1.41 us

profile of v2, /device:TPU:0, one launch (start us, length us, event | category | flops | bytes accessed | tf_op | source)
XLA Modules:
  0.0 31.9 jit_solution(12956876763581545107)
XLA Ops:
  0.6 29.9 %shard_map.68 = (f32[16,512]{1,0:T(8,128)S(1)}, bf16[1024,256]{1,0:T(8,128)(2,1)S(1)}) custom-call(bf16[4096,128]{1,0:T(8,128)(2,1)} %snap.1, s32[1,128]{1,0:T(1,128)} %bitcast.4, s32[1,128]{1,0:T(1,128)} %bitcast.5, bf16[40,128]{1,0:T(8,128)(2,1)} %bitcast.3, bf16[128,256]{1,0:T(8,128)(2,1)} %panels.1), custom_call_target="tpu_custom_call" | custom-call | tf_op jit(solution)/shard_map/pallas_call | solution.py:303
  30.5 0.6 %copy.9 = f32[16,512]{1,0:T(8,128)} copy(f32[16,512]{1,0:T(8,128)S(1)} %get-tuple-element.4) | data formatting | bytes 65536
  31.1 0.8 %copy.10 = bf16[1024,256]{1,0:T(8,128)(2,1)} copy(bf16[1024,256]{1,0:T(8,128)(2,1)S(1)} %get-tuple-element.5) | data formatting | bytes 1048576

commit v3 on v2

--- a/solution.py
+++ b/solution.py
@@ -72,7 +72,7 @@
     gram_out, modes_out,
     starts, widths, coeffs,
     packed, weights, gathered, resampled, acc, pair_in, mine32, tm_out, tm_in, z_out, z_in, panel_all,
-    local_sem, pack_send, pack_recv, row_send, row_recv, panel_send, panel_recv,
+    local_sem, pack_send, pack_recv, row_send, row_recv, panel_send, panel_recv, relay_send, relay_recv,
     pair_send, pair_recv, tm_send, tm_recv, z_send, z_recv,
 ):
     space = lax.axis_index("space")
@@ -88,9 +88,14 @@
     def at(space_id, tm_id):
         return dict(device_id=(space_id, tm_id), device_id_type=pl.DeviceIdType.MESH)
 
-    tm_peers = [lax.rem(t + d, ntm) for d in range(1, ntm)]
+    tm_peers = [t ^ mask for mask in range(ntm - 1, 0, -1)]
     z_peers = [lax.rem(zz + d, nz) * CORES + core for d in range(1, nz)]
     partner = zz * CORES + (1 - core)
+
+    half = block // CORES
+
+    def share_of(tm_id, core_id=core):
+        return pl.ds(pl.multiple_of(tm_id * block + core_id * half, half), half)
 
     barrier = pltpu.get_barrier_semaphore()
     for peer in z_peers:
@@ -146,7 +151,9 @@
                 gathered.at[pl.ds(c * piece, piece), columns],
                 row_send.at[c, i], row_recv.at[c, i], space, peer)
     for i, peer in enumerate(tm_peers):
-        send(panels, panel_all.at[columns, :], panel_send.at[i], panel_recv.at[i], space, peer)
+        send(
+            panels.at[pl.ds(pl.multiple_of(core * half, half), half), :], panel_all.at[share_of(t), :],
+            panel_send.at[i], panel_recv.at[i], space, peer)
 
     weights[...] = jnp.zeros_like(weights)
     acc[...] = jnp.zeros_like(acc)
@@ -156,9 +163,7 @@
             src_ref=dst, dst_ref=dst, send_sem=sem, recv_sem=sem, **at(space, tm_peers[0])
         ).wait_recv()
 
-    origins = [lax.rem(t + ntm - d, ntm) for d in range(1, ntm)]
-
-    for i, origin in enumerate(origins):
+    for i, origin in enumerate(tm_peers):
         arrived(packed.at[origin], pack_recv.at[i])
     for b in range(ntm):
         value = spread(packed[b], width_max, block).astype(BF16)
@@ -170,7 +175,7 @@
 
     def resample(c):
         at_rows = pl.ds(pl.multiple_of(c * piece, piece), piece)
-        for i, origin in enumerate(origins):
+        for i, origin in enumerate(tm_peers):
             arrived(
                 gathered.at[at_rows, pl.ds(pl.multiple_of(origin * block, block), block)], row_recv.at[c, i]
             )
@@ -210,17 +215,11 @@
                 tm_out.at[peer, :, :, part], tm_in.at[i, :, :, part],
                 tm_send.at[h, i], tm_recv.at[h, i], space, peer)
 
-    own_panels.wait()
-    for i, origin in enumerate(origins):
-        arrived(panel_all.at[pl.ds(pl.multiple_of(origin * block, block), block), :], panel_recv.at[i])
-
-    def modes_step(c, carry):
-        at_rows = pl.ds(pl.multiple_of(c * piece, piece), piece)
-        modes_out[at_rows, :] = jnp.dot(
-            resampled[at_rows, :], panel_all[...], preferred_element_type=F32).astype(BF16)
-        return carry
-
-    lax.fori_loop(0, chunks, modes_step, 0)
+    for i, origin in enumerate(tm_peers):
+        arrived(panel_all.at[share_of(origin), :], panel_recv.at[i])
+        send(
+            panel_all.at[share_of(origin), :], panel_all.at[share_of(origin), :],
+            relay_send.at[i], relay_recv.at[i], partner, t)
 
     for h, part in enumerate(parts):
         total = mine32[pl.ds(t, 1), :, :, part].reshape(z_out.shape[:2] + (wide,))
@@ -233,6 +232,18 @@
             send(
                 z_out.at[lax.rem(zz + i + 1, nz), :, part], z_in.at[i, :, part],
                 z_send.at[h, i], z_recv.at[h, i], peer, t)
+    own_panels.wait()
+    for i, origin in enumerate(tm_peers):
+        arrived(panel_all.at[share_of(origin, 1 - core), :], relay_recv.at[i])
+
+    def modes_step(c, carry):
+        at_rows = pl.ds(pl.multiple_of(c * piece, piece), piece)
+        modes_out[at_rows, :] = jnp.dot(
+            resampled[at_rows, :], panel_all[...], preferred_element_type=F32).astype(BF16)
+        return carry
+
+    lax.fori_loop(0, chunks, modes_step, 0)
+
     for h, part in enumerate(parts):
         final = mine32[pl.ds(t, 1), pl.ds(zz, 1), :, part].reshape(gram_out.shape[0], wide)
         for i in range(nz - 1):
@@ -286,6 +297,8 @@
             dma((chunks, ntm - 1)),
             dma((ntm - 1,)),
             dma((ntm - 1,)),
+            dma((ntm - 1,)),
+            dma((ntm - 1,)),
             dma((halves,)),
             dma((halves,)),
             dma((halves, ntm - 1)),
@@ -300,7 +313,25 @@
     operands = (
         snapshots, stencil_starts.reshape(1, block), stencil_widths.reshape(1, block), stencil_coeffs.T, panels
     )
-    return call(*(pltpu.with_memory_space_constraint(operand, pltpu.HBM) for operand in operands))
+    values = call(*(pltpu.with_memory_space_constraint(operand, pltpu.HBM) for operand in operands))
+    return pl.pallas_call(
+        store,
+        out_shape=tuple(jax.ShapeDtypeStruct(value.shape, value.dtype) for value in values),
+        in_specs=[vmem, vmem],
+        out_specs=(hbm, hbm),
+        scratch_shapes=[dma((2,))],
+    )(*(pltpu.with_memory_space_constraint(value, pltpu.VMEM) for value in values))
+
+
+def store(gram, modes, gram_out, modes_out, sem):
+    copies = [
+        pltpu.make_async_copy(modes, modes_out, sem.at[0]),
+        pltpu.make_async_copy(gram, gram_out, sem.at[1]),
+    ]
+    for copy in copies:
+        copy.start()
+    for copy in copies:
+        copy.wait()
 
 
 def solution(mesh):
@@ -309,7 +340,7 @@
     def body(snapshots, stencil_starts, stencil_widths, stencil_coeffs, panels):
         rows, block = snapshots.shape
         own = block // nsp
-        fits = block == 128 and own % 16 == 0 and nsp % CORES == 0 and ntm % 2 == 0 and rows % (64 * ntm) == 0
+        fits = block == 128 and own % 16 == 0 and nsp % CORES == 0 and ntm % 2 == 0 and ntm & (ntm - 1) == 0 and rows % (64 * ntm) == 0
         if fits and 4 * (block * ntm) ** 2 <= 4 * 1024 * 1024:
             return fused(nsp, ntm, snapshots, stencil_starts, stencil_widths, stencil_coeffs, panels)
         return on_device(snapshots, stencil_starts, stencil_widths, stencil_coeffs, panels)

time: 32.1 us -> 30.9 us (0.963)
  local copies, waits for them, and re-layouts: 1.41 us -> 0 us
    unnamed x2 -> x0, local copies, waits for them, and re-layouts: 1.41 us -> none
    pallas_call x0 -> x1, Pallas kernels: none -> 0.81 us  [fused(): pl.pallas_call(store, out_shape=tuple((jax.ShapeDtypeStruct(value.shape,...]
    pallas_call x1, Pallas kernels: 29.9 us -> 29.3 us  [fused(): call(*(pltpu.with_memory_space_constraint(operand, pltpu.HBM) for operand...]
where the time goes in v3:
time: 30.9 us; the launch traced here: 30.7 us
  Pallas kernels  30.1 us (97%)
  between operations  0.64 us (2%)
    pallas_call x1, Pallas kernels, fused(): call(*(pltpu.with_memory_space_constraint(operand, pltpu.HBM) for operand...  29.3 us
    pallas_call x1, Pallas kernels, fused(): pl.pallas_call(store, out_shape=tuple((jax.ShapeDtypeStruct(value.shape,...  0.81 us

profile of v3, /device:TPU:0, one launch (start us, length us, event | category | flops | bytes accessed | tf_op | source)
XLA Modules:
  0.0 30.7 jit_solution(8371111457000126735)
XLA Ops:
  0.6 29.3 %shard_map.68 = (f32[16,512]{1,0:T(8,128)S(1)}, bf16[1024,256]{1,0:T(8,128)(2,1)S(1)}) custom-call(bf16[4096,128]{1,0:T(8,128)(2,1)} %snap.1, s32[1,128]{1,0:T(1,128)} %bitcast.4, s32[1,128]{1,0:T(1,128)} %bitcast.5, bf16[40,128]{1,0:T(8,128)(2,1)} %bitcast.3, bf16[128,256]{1,0:T(8,128)(2,1)} %panels.1), custom_call_target="tpu_custom_call" | custom-call | tf_op jit(solution)/shard_map/pallas_call | solution.py:316
  29.9 0.8 %shard_map.69 = (f32[16,512]{1,0:T(8,128)}, bf16[1024,256]{1,0:T(8,128)(2,1)}) custom-call(f32[16,512]{1,0:T(8,128)S(1)} %get-tuple-element.4.gram, bf16[1024,256]{1,0:T(8,128)(2,1)S(1)} %get-tuple-element.5.modes), custom_call_target="tpu_custom_call" | custom-call | tf_op jit(solution)/shard_map/pallas_call | solution.py:317

commit v4 on v3

--- a/solution.py
+++ b/solution.py
@@ -72,7 +72,7 @@
     gram_out, modes_out,
     starts, widths, coeffs,
     packed, weights, gathered, resampled, acc, pair_in, mine32, tm_out, tm_in, z_out, z_in, panel_all,
-    local_sem, pack_send, pack_recv, row_send, row_recv, panel_send, panel_recv, relay_send, relay_recv,
+    local_sem, pack_send, pack_recv, row_send, row_recv, panel_send, panel_recv, relay_send, relay_recv, hand_send, hand_recv,
     pair_send, pair_recv, tm_send, tm_recv, z_send, z_recv,
 ):
     space = lax.axis_index("space")
@@ -97,6 +97,10 @@
     def share_of(tm_id, core_id=core):
         return pl.ds(pl.multiple_of(tm_id * block + core_id * half, half), half)
 
+    def table_of(tm_id, core_id=core):
+        rows = packed.shape[1] // CORES
+        return packed.at[tm_id, pl.ds(pl.multiple_of(core_id * rows, rows), rows), :]
+
     barrier = pltpu.get_barrier_semaphore()
     for peer in z_peers:
         pl.semaphore_signal(barrier, inc=1, **at(peer, t))
@@ -143,7 +147,7 @@
         sends.append(copy)
 
     for i, peer in enumerate(tm_peers):
-        send(packed.at[t], packed.at[t], pack_send.at[i], pack_recv.at[i], space, peer)
+        send(table_of(t), table_of(t), pack_send.at[i], pack_recv.at[i], space, peer)
     for c in range(chunks):
         for i, peer in enumerate(tm_peers):
             send(
@@ -164,7 +168,10 @@
         ).wait_recv()
 
     for i, origin in enumerate(tm_peers):
-        arrived(packed.at[origin], pack_recv.at[i])
+        arrived(table_of(origin), pack_recv.at[i])
+        send(table_of(origin), table_of(origin), hand_send.at[i], hand_recv.at[i], partner, t)
+    for i, origin in enumerate(tm_peers):
+        arrived(table_of(origin, 1 - core), hand_recv.at[i])
     for b in range(ntm):
         value = spread(packed[b], width_max, block).astype(BF16)
         height = min(value.shape[0], nu - b * block)
@@ -262,7 +269,7 @@
     nu, share, nz = block * ntm, rows // ntm, nsp // CORES
     own = nu // (ntm * nsp)
     chunks, halves = CHUNKS, 2
-    prow = -(-(width_max + 1) // 16) * 16
+    prow = -(-(width_max + 1) // 32) * 32
     vmem = pl.BlockSpec(memory_space=pltpu.VMEM)
     hbm = pl.BlockSpec(memory_space=pltpu.HBM)
     dma = pltpu.SemaphoreType.DMA
@@ -299,6 +306,8 @@
             dma((ntm - 1,)),
             dma((ntm - 1,)),
             dma((ntm - 1,)),
+            dma((ntm - 1,)),
+            dma((ntm - 1,)),
             dma((halves,)),
             dma((halves,)),
             dma((halves, ntm - 1)),

time: 30.9 us -> 30.8 us (level)
  no operation moved by 1% of the time
where the time goes in v4:
time: 30.8 us; the launch traced here: 30.7 us
  Pallas kernels  30 us (97%)
  between operations  0.64 us (2%)
    pallas_call x1, Pallas kernels, fused(): call(*(pltpu.with_memory_space_constraint(operand, pltpu.HBM) for operand...  29.2 us
    pallas_call x1, Pallas kernels, fused(): pl.pallas_call(store, out_shape=tuple((jax.ShapeDtypeStruct(value.shape,...  0.81 us

profile of v4, /device:TPU:0, one launch (start us, length us, event | category | flops | bytes accessed | tf_op | source)
XLA Modules:
  0.0 30.7 jit_solution(16225068616583139325)
XLA Ops:
  0.6 29.2 %shard_map.68 = (f32[16,512]{1,0:T(8,128)S(1)}, bf16[1024,256]{1,0:T(8,128)(2,1)S(1)}) custom-call(bf16[4096,128]{1,0:T(8,128)(2,1)} %snap.1, s32[1,128]{1,0:T(1,128)} %bitcast.4, s32[1,128]{1,0:T(1,128)} %bitcast.5, bf16[40,128]{1,0:T(8,128)(2,1)} %bitcast.3, bf16[128,256]{1,0:T(8,128)(2,1)} %panels.1), custom_call_target="tpu_custom_call" | custom-call | tf_op jit(solution)/shard_map/pallas_call | solution.py:325
  29.8 0.8 %shard_map.69 = (f32[16,512]{1,0:T(8,128)}, bf16[1024,256]{1,0:T(8,128)(2,1)}) custom-call(f32[16,512]{1,0:T(8,128)S(1)} %get-tuple-element.4.gram, bf16[1024,256]{1,0:T(8,128)(2,1)S(1)} %get-tuple-element.5.modes), custom_call_target="tpu_custom_call" | custom-call | tf_op jit(solution)/shard_map/pallas_call | solution.py:326
